TPU v7x, 32 devices: a whole 2x2x4 slice. The times are simulated.
32 devices in a mesh: pix: 4 (over y, core), chan: 8 (over z, x).
Axes of the slice: x: 2, y: 2, z: 4, core: 2. Of those that a mesh axis runs over, the one named last changes fastest.
Arguments:
- images: bfloat16 [2048, 32, 128], P('pix', 'chan'), may hold values from -6 to 6
- conv_weight: float32 [2048, 49], P('pix'), may hold values from -6 to 6
- conv_bias: float32 [2048], P('pix'), may hold values from -4 to 4
- norm_gain: float32 [2048], replicated, may hold values from 0.25 to 1.75
- norm_shift: float32 [2048], replicated, may hold values from -3 to 3
- up_weight: bfloat16 [2048, 8192], P(None, 'pix'), may hold values from -0.125 to 0.125
- up_bias: float32 [8192], P('pix'), may hold values from -3 to 3
- down_weight: bfloat16 [2048, 8192], P(None, 'pix'), may hold values from -0.09375 to 0.09375
- down_bias: float32 [2048], P('pix'), may hold values from -3 to 3
- layer_scale: float32 [2048], P('pix'), may hold values from 0.5 to 2
Outputs:
- block_out: bfloat16 [2048, 32, 128], P('pix', 'chan')
All inputs are finite; a program needn't handle non-finite values.
Results may differ from a plain program's by a relative error of at most 0.006.
Values may be sent and summed in bfloat16 or wider, within the bound.
A program may use at most 64 MiB of HBM per device.

v0:
```python
import jax
import jax.numpy as jnp
from jax import lax
from jax.sharding import PartitionSpec as P

C = 2048


def with_halo(block, sides, width):
    for axis, dim in sides:
        count = lax.axis_size(axis)
        forward = [(i, i + 1) for i in range(count - 1)]
        backward = [(target, source) for source, target in forward]
        low = lax.ppermute(
            lax.slice_in_dim(block, block.shape[dim] - width, None, axis=dim), axis, forward
        )
        high = lax.ppermute(lax.slice_in_dim(block, 0, width, axis=dim), axis, backward)
        block = jnp.concatenate([low, block, high], axis=dim)
    return block


def on_device(
    images,
    conv_weight,
    conv_bias,
    norm_gain,
    norm_shift,
    up_weight,
    up_bias,
    down_weight,
    down_bias,
    layer_scale,
):
    chans, rows, width = images.shape
    pixels = rows * width
    padded = with_halo(images, (("chan", 1),), 3)
    wide = jnp.pad(padded.astype(jnp.float32), ((0, 0), (0, 0), (3, 3)))
    total = jnp.zeros((chans, rows, width), jnp.float32)
    for first in range(7):
        for second in range(7):
            total = (
                total
                + conv_weight[:, first * 7 + second][:, None, None]
                * wide[:, first : first + rows, second : second + width]
            )
    filtered = (total + conv_bias[:, None, None]).astype(jnp.bfloat16).reshape(chans, pixels)
    values = filtered.astype(jnp.float32)
    sum_first, sum_second = lax.psum(
        (jnp.sum(values, axis=0), jnp.sum(values * values, axis=0)), "pix"
    )
    mean = sum_first / C
    var = sum_second / C - mean * mean
    offset = lax.axis_index("pix") * chans
    gain_local = lax.dynamic_slice_in_dim(norm_gain, offset, chans, 0)
    shift_local = lax.dynamic_slice_in_dim(norm_shift, offset, chans, 0)
    normed_local = (
        (values - mean) * lax.rsqrt(var + 1e-06) * gain_local[:, None] + shift_local[:, None]
    ).astype(jnp.bfloat16)
    gathered = lax.all_gather(normed_local, "pix", axis=0, tiled=True)
    contract = (((0,), (0,)), ((), ()))
    pre = lax.dot_general(up_weight, gathered, contract, preferred_element_type=jnp.float32)
    hidden = jax.nn.gelu(pre + up_bias[:, None], approximate=True).astype(jnp.bfloat16)
    terms = jnp.dot(down_weight, hidden, preferred_element_type=jnp.float32)
    mixed = lax.psum_scatter(terms, "pix", scatter_dimension=0, tiled=True)
    result = images.astype(jnp.float32).reshape(chans, pixels) + layer_scale[:, None] * (
        mixed + down_bias[:, None]
    )
    return result.astype(jnp.bfloat16).reshape(chans, rows, width)


def solution(mesh):
    placed = (
        P("pix", "chan", None),
        P("pix", None),
        P("pix"),
        P(),
        P(),
        P(None, "pix"),
        P("pix"),
        P(None, "pix"),
        P("pix"),
        P("pix"),
    )
    return jax.shard_map(
        on_device, mesh=mesh, in_specs=placed, out_specs=P("pix", "chan", None), check_vma=False
    )
```

profile of v0, /device:TPU:0, one launch (start us, length us, event | category | flops | bytes accessed | tf_op | source)
XLA Modules:
  0.0 194.6 jit_solution(2396810698593595446)
XLA Ops:
  6.5 0.0 copy-start.3
  6.5 0.0 all-gather.2.cloned.1.call-start
  6.5 1.7 fusion.103
  8.2 4.9 %collective-permute-start = (bf16[512,3,128]{2,1,0:T(4,128)(2,1)S(1)}, bf16[512,3,128]{2,1,0:T(4,128)(2,1)S(1)}, u32[]{:S(2)}, u32[]{:S(2)}) collective-permute-start(bf16[512,3,128]{2,1,0:T(4,128)(2,1)S(1)} %get-tuple-element.10), channel_id=1, source_target_pairs={{0,1},{1,2},{2,3},{3,4},{4,5},{5,6},{6,7},{8,9},{9,10},{10,11},{11... | collective-permute-start | bytes 1179656 | tf_op jit(solution)/shard_map/ppermute | solution.py:14
  13.1 1.3 collective-permute-start.1
  14.5 1.1 fusion.104
  15.6 0.8 dynamic_slice.6
  16.4 0.8 dynamic_slice.7
  17.1 1.0 fusion.106
  18.1 1.2 fusion.105
  19.2 16.3 %collective-permute-done = bf16[512,3,128]{2,1,0:T(4,128)(2,1)S(1)} collective-permute-done((bf16[512,3,128]{2,1,0:T(4,128)(2,1)S(1)}, bf16[512,3,128]{2,1,0:T(4,128)(2,1)S(1)}, u32[]{:S(2)}, u32[]{:S(2)}) %collective-permute-start) | collective-permute-done | bytes 393248 | tf_op jit(solution)/shard_map/ppermute | solution.py:14
  35.5 0.0 collective-permute-done.1
  35.5 2.2 %maximum_convert_fusion = f32[512,10,128]{2,1,0:T(8,128)S(1)} fusion(bf16[512,3,128]{2,1,0:T(4,128)(2,1)S(1)} %collective-permute-done.1, bf16[512,4,128]{2,1,0:T(4,128)(2,1)} %param.10, bf16[512,3,128]{2,1,0:T(4,128)(2,1)S(1)} %collective-permute-done), kind=kLoop, calls=%fused_computation.52 | loop fusion | flops 3932160 | bytes 3932160 | tf_op jit(solution)/shard_map/convert_element_type | solution.py:37
  37.7 0.0 copy-done.3
  37.7 0.0 copy-start.4
  37.7 52.7 %convert_reduce_fusion = (f32[4,128]{1,0:T(4,128)S(1)}, f32[4,128]{1,0:T(4,128)S(1)}, bf16[512,4,128]{2,1,0:T(4,128)(2,1)S(1)}) fusion(f32[512]{0:T(512)S(1)} %copy-done.3, f32[512]{0:T(512)S(1)} %bitcast.118, f32[512]{0:T(512)S(1)} %bitcast.119, f32[512]{0:T(512)S(1)} %bitcast.91, f32[512,10,128]{2,1,0:T(8,128)S(1)} %maximum_convert_fusion, ...), kind=kLoop, calls=%fused_computation.159 | loop fusion | flops 26999808 | bytes 12165120 | tf_op jit(solution)/shard_map/reduce_sum | solution.py:49
  90.4 0.1 convert.2
  90.6 5.8 %all-reduce.1 = (f32[512]{0:T(512)S(1)}, f32[512]{0:T(512)S(1)}) all-reduce(f32[512]{0:T(512)S(1)} %bitcast.140, f32[512]{0:T(512)S(1)} %bitcast.139), channel_id=1, replica_groups=mesh['pix'=4,'chan'=8] {'pix'}, use_global_device_ids=true, to_apply=%region_3.4 | all-reduce | flops 1024 | bytes 8192 | tf_op jit(solution)/shard_map/psum | solution.py:48
  96.3 1.0 fusion.101
  97.4 0.0 all-gather.2.cloned.1.call-update
  97.4 0.2 reduce-scatter.2.cloned.1.call-start
  97.6 24.9 %all-gather.2.cloned.1.call-done = bf16[2048,512]{1,0:T(8,128)(2,1)} async-done(((bf16[512,512]{1,0:T(8,128)(2,1)}), bf16[2048,512]{1,0:T(8,128)(2,1)}) %all-gather.2.cloned.1.call-update) | async-done | bytes 2097168 | tf_op jit(solution)/shard_map/all_gather | solution.py:59
  122.5 0.0 copy-done.4
  122.5 18.1 %convolution_bitcast_fusion = f32[2048,512]{0,1:T(8,128)} fusion(bf16[2048,2048]{1,0:T(8,128)(2,1)} %param.17, bf16[2048,512]{1,0:T(8,128)(2,1)} %all-gather.2.cloned.1.call-done, bf16[2048,2048]{1,0:T(8,128)(2,1)} %param.15, f32[2048]{0:T(1024)S(1)} %copy-done.4), kind=kOutput, calls=%fused_computation.51 | convolution fusion | flops 8600420352 | bytes 23076864 | tf_op jit(solution)/shard_map/dot_general | solution.py:63
  140.6 0.0 copy-start
  140.6 0.0 copy-start.1
  140.6 0.0 copy-start.2
  140.6 0.0 reduce-scatter.2.cloned.1.call-update
  140.6 1.0 copy-done
  141.6 0.3 copy.11
  141.9 43.2 %reduce-scatter.2.cloned.1.call-done = f32[512,512]{0,1:T(8,128)} async-done(((f32[2048,512]{0,1:T(8,128)}), f32[512,512]{0,1:T(8,128)}) %reduce-scatter.2.cloned.1.call-update) | async-done | bytes 1048592 | tf_op jit(solution)/shard_map/reduce_scatter | solution.py:64
  185.2 0.0 copy-done.1
  185.2 0.0 copy-done.2
  185.2 1.5 fusion.102
  186.6 1.1 copy.12
  (1 shorter events, 0.0 us)
Async XLA Ops:
  6.5 31.2 %copy-start.3 = (f32[512]{0:T(512)S(1)}, f32[512]{0:T(512)}, u32[]{:S(2)}) copy-start(f32[512]{0:T(512)} %param.12) | copy-start | bytes 6148
  6.5 116.0 %all-gather.2.cloned.1.call-start = ((), (), s32[]{:S(2)}) async-start(), calls=%async_computation.1 | async-start | bytes 2621440 | tf_op jit(solution)/shard_map/all_gather | solution.py:59
  8.2 27.3 %collective-permute-start = (bf16[512,3,128]{2,1,0:T(4,128)(2,1)S(1)}, bf16[512,3,128]{2,1,0:T(4,128)(2,1)S(1)}, u32[]{:S(2)}, u32[]{:S(2)}) collective-permute-start(bf16[512,3,128]{2,1,0:T(4,128)(2,1)S(1)} %get-tuple-element.10), channel_id=1, source_target_pairs={{0,1},{1,2},{2,3},{3,4},{4,5},{5,6},{6,7},{8,9},{9,10},{10,11},{11... | collective-permute-start | bytes 1179656 | tf_op jit(solution)/shard_map/ppermute | solution.py:14
  13.1 22.4 %collective-permute-start.1 = (bf16[512,3,128]{2,1,0:T(4,128)(2,1)S(1)}, bf16[512,3,128]{2,1,0:T(4,128)(2,1)S(1)}, u32[]{:S(2)}, u32[]{:S(2)}) collective-permute-start(bf16[512,3,128]{2,1,0:T(4,128)(2,1)S(1)} %get-tuple-element.11), channel_id=1, source_target_pairs={{1,0},{2,1},{3,2},{4,3},{5,4},{6,5},{7,6},{9,8},{10,9},{11,10},{12... | collective-permute-start | bytes 1179656 | tf_op jit(solution)/shard_map/ppermute | solution.py:17
  37.7 84.8 %copy-start.4 = (f32[2048]{0:T(1024)S(1)}, f32[2048]{0:T(1024)}, u32[]{:S(2)}) copy-start(f32[2048]{0:T(1024)} %param.16) | copy-start | bytes 24580
  97.4 87.8 %reduce-scatter.2.cloned.1.call-start = ((), (), s32[]{:S(2)}) async-start(), calls=%async_computation.2 | async-start | bytes 5242880 | tf_op jit(solution)/shard_map/reduce_scatter | solution.py:64
  140.6 1.0 copy-start
  140.6 44.6 %copy-start.1 = (f32[512]{0:T(512)S(1)}, f32[512]{0:T(512)}, u32[]{:S(2)}) copy-start(f32[512]{0:T(512)} %param.18) | copy-start | bytes 6148
  140.6 44.6 %copy-start.2 = (f32[512]{0:T(512)S(1)}, f32[512]{0:T(512)}, u32[]{:S(2)}) copy-start(f32[512]{0:T(512)} %param.19) | copy-start | bytes 6148
Sparse Core Ops, SparseCore 0:
  97.5 24.9 all-gather.1
  140.7 44.3 reduce-scatter.1
where the time goes:
time: 195 us
  waiting for transfers between devices  84.4 us (43%)
  other arithmetic  57.5 us (29%)
  matrix products  18.1 us (9%)
  between operations  13.5 us (7%)
  local copies, waits for them, and re-layouts  8.88 us (5%)
  starting transfers between devices  6.42 us (3%)
  blocking collectives  5.76 us (3%)
    reduce_sum x1, other arithmetic, on_device(): jnp.sum(values, axis=0)  52.7 us
    reduce_scatter x1, waiting for transfers between devices, on_device(): mixed = lax.psum_scatter(terms, 'pix', scatter_dimension=0, tiled=True)  43.2 us
    all_gather x1, waiting for transfers between devices, on_device(): gathered = lax.all_gather(normed_local, 'pix', axis=0, tiled=True)  24.9 us
    dot_general x1, matrix products, on_device(): terms = jnp.dot(down_weight, hidden, preferred_element_type=jnp.float32)  18.1 us
    ppermute x1, waiting for transfers between devices, with_halo(): lax.ppermute(lax.slice_in_dim(block, block.shape[dim] - width, None, axis...  16.3 us
    psum x1, blocking collectives, on_device(): lax.psum((jnp.sum(values, axis=0), jnp.sum(values * values, axis=0)), 'pix')  5.76 us
    ppermute x1, starting transfers between devices, with_halo(): lax.ppermute(lax.slice_in_dim(block, block.shape[dim] - width, None, axis...  4.9 us
  transfers between devices with their start and end apart: 4, of which 3 were waited for; matrix products, arithmetic and copies ran while one was open for 3% of the time, Pallas kernels for 0%

commit v1 on v0

--- a/solution.py
+++ b/solution.py
@@ -56,7 +56,23 @@
     normed_local = (
         (values - mean) * lax.rsqrt(var + 1e-06) * gain_local[:, None] + shift_local[:, None]
     ).astype(jnp.bfloat16)
-    gathered = lax.all_gather(normed_local, "pix", axis=0, tiled=True)
+
+    def lay_islands(patch, axis_id):
+        cores_n = lax.psum(1, axis_id)
+        heap = [patch]
+        hop_no = 1
+        while hop_no < cores_n:
+            heap.append(
+                lax.ppermute(
+                    heap[hop_no - 1], axis_id, [(d, (d - 1) % cores_n) for d in range(cores_n)]
+                )
+            )
+            hop_no = hop_no + 1
+        work_now = jnp.concatenate(heap, axis=0)
+        block_last = jnp.roll(work_now, lax.axis_index(axis_id) * patch.shape[0], axis=0)
+        return block_last
+
+    gathered = lay_islands(normed_local, "pix")
     contract = (((0,), (0,)), ((), ()))
     pre = lax.dot_general(up_weight, gathered, contract, preferred_element_type=jnp.float32)
     hidden = jax.nn.gelu(pre + up_bias[:, None], approximate=True).astype(jnp.bfloat16)

time: 195 us -> 202 us (1.036)
  local copies, waits for them, and re-layouts: 8.88 us -> 14.8 us
  starting transfers between devices: 6.42 us -> 10.9 us
  waiting for transfers between devices: 84.4 us -> 80.8 us
    all_gather x1 -> x0, waiting for transfers between devices: 24.9 us -> none  [on_device(): gathered = lax.all_gather(normed_local, 'pix', axis=0, tiled=True)]
    ppermute x0 -> x3, waiting for transfers between devices: none -> 18.4 us  [lay_islands(): lax.ppermute(heap[hop_no - 1], axis_id, [(d, (d - 1) % cores_n) for d in...]
    unnamed x10 -> x16, local copies, waits for them, and re-layouts: 1.03 us -> 6.04 us
    ppermute x0 -> x3, starting transfers between devices: none -> 4.71 us  [lay_islands(): lax.ppermute(heap[hop_no - 1], axis_id, [(d, (d - 1) % cores_n) for d in...]
    reduce_scatter x1, waiting for transfers between devices: 43.2 us -> 46.1 us  [on_device(): mixed = lax.psum_scatter(terms, 'pix', scatter_dimension=0, tiled=True)]
  transfers between devices with their start and end apart: 4 -> 6, of which waited for: 3 -> 5; matrix products, arithmetic and copies ran while one was open for 3% -> 3% of each run, Pallas kernels for 0% -> 0%
where the time goes in v1:
time: 202 us; the launch traced here: 201 us
  waiting for transfers between devices  80.8 us (40%)
  other arithmetic  57.5 us (28%)
  matrix products  18.1 us (9%)
  local copies, waits for them, and re-layouts  14.8 us (7%)
  between operations  13.5 us (7%)
  starting transfers between devices  10.9 us (5%)
  blocking collectives  5.76 us (3%)
    reduce_sum x1, other arithmetic, on_device(): jnp.sum(values, axis=0)  52.7 us
    reduce_scatter x1, waiting for transfers between devices, on_device(): mixed = lax.psum_scatter(terms, 'pix', scatter_dimension=0, tiled=True)  46.1 us
    ppermute x3, waiting for transfers between devices, lay_islands(): lax.ppermute(heap[hop_no - 1], axis_id, [(d, (d - 1) % cores_n) for d in...  18.4 us
    dot_general x1, matrix products, on_device(): terms = jnp.dot(down_weight, hidden, preferred_element_type=jnp.float32)  18.1 us
    ppermute x1, waiting for transfers between devices, with_halo(): lax.ppermute(lax.slice_in_dim(block, block.shape[dim] - width, None, axis...  16.3 us
    unnamed x16, local copies, waits for them, and re-layouts  6.04 us
    psum x1, blocking collectives, on_device(): lax.psum((jnp.sum(values, axis=0), jnp.sum(values * values, axis=0)), 'pix')  5.76 us
    ppermute x1, starting transfers between devices, with_halo(): lax.ppermute(lax.slice_in_dim(block, block.shape[dim] - width, None, axis...  4.9 us
  transfers between devices with their start and end apart: 6, of which 5 were waited for; matrix products, arithmetic and copies ran while one was open for 3% of the time, Pallas kernels for 0%

profile of v1, /device:TPU:0, one launch (start us, length us, event | category | flops | bytes accessed | tf_op | source)
XLA Modules:
  0.0 201.4 jit_solution(1766036209078017531)
XLA Ops:
  6.5 0.0 copy-start.3
  6.5 0.0 reduce-scatter.2.cloned.1.call-start
  6.5 1.7 fusion.113
  8.2 4.9 %collective-permute-start = (bf16[512,3,128]{2,1,0:T(4,128)(2,1)S(1)}, bf16[512,3,128]{2,1,0:T(4,128)(2,1)S(1)}, u32[]{:S(2)}, u32[]{:S(2)}) collective-permute-start(bf16[512,3,128]{2,1,0:T(4,128)(2,1)S(1)} %get-tuple-element.12), channel_id=1, source_target_pairs={{0,1},{1,2},{2,3},{3,4},{4,5},{5,6},{6,7},{8,9},{9,10},{10,11},{11... | collective-permute-start | bytes 1179656 | tf_op jit(solution)/shard_map/ppermute | solution.py:14
  13.1 1.3 collective-permute-start.1
  14.5 1.1 fusion.114
  15.6 0.8 dynamic_slice.10
  16.4 0.8 dynamic_slice.11
  17.1 1.0 fusion.116
  18.1 1.2 fusion.115
  19.2 16.3 %collective-permute-done = bf16[512,3,128]{2,1,0:T(4,128)(2,1)S(1)} collective-permute-done((bf16[512,3,128]{2,1,0:T(4,128)(2,1)S(1)}, bf16[512,3,128]{2,1,0:T(4,128)(2,1)S(1)}, u32[]{:S(2)}, u32[]{:S(2)}) %collective-permute-start) | collective-permute-done | bytes 393248 | tf_op jit(solution)/shard_map/ppermute | solution.py:14
  35.5 0.0 collective-permute-done.1
  35.5 2.2 %maximum_convert_fusion = f32[512,10,128]{2,1,0:T(8,128)S(1)} fusion(bf16[512,3,128]{2,1,0:T(4,128)(2,1)S(1)} %collective-permute-done.1, bf16[512,4,128]{2,1,0:T(4,128)(2,1)} %param.10, bf16[512,3,128]{2,1,0:T(4,128)(2,1)S(1)} %collective-permute-done), kind=kLoop, calls=%fused_computation.52 | loop fusion | flops 3932160 | bytes 3932160 | tf_op jit(solution)/shard_map/convert_element_type | solution.py:37
  37.7 0.0 copy-done.3
  37.7 52.7 %convert_reduce_fusion = (f32[4,128]{1,0:T(4,128)S(1)}, f32[4,128]{1,0:T(4,128)S(1)}, bf16[512,4,128]{2,1,0:T(4,128)(2,1)S(1)}) fusion(f32[512]{0:T(512)S(1)} %copy-done.3, f32[512]{0:T(512)S(1)} %bitcast.107, f32[512]{0:T(512)S(1)} %bitcast.108, f32[512]{0:T(512)S(1)} %bitcast.80, f32[512,10,128]{2,1,0:T(8,128)S(1)} %maximum_convert_fusion, ...), kind=kLoop, calls=%fused_computation.160 | loop fusion | flops 26999808 | bytes 12165120 | tf_op jit(solution)/shard_map/reduce_sum | solution.py:49
  90.4 0.1 convert.2
  90.6 5.8 %all-reduce.1 = (f32[512]{0:T(512)S(1)}, f32[512]{0:T(512)S(1)}) all-reduce(f32[512]{0:T(512)S(1)} %bitcast.129, f32[512]{0:T(512)S(1)} %bitcast.128), channel_id=1, replica_groups=mesh['pix'=4,'chan'=8] {'pix'}, use_global_device_ids=true, to_apply=%region_3.4 | all-reduce | flops 1024 | bytes 8192 | tf_op jit(solution)/shard_map/psum | solution.py:48
  96.3 1.0 constant_dynamic-update-slice_fusion.7
  97.4 0.0 copy-start.4
  97.4 0.9 collective-permute-start.2
  98.3 6.7 %collective-permute-done.2 = bf16[512,512]{1,0:T(8,128)(2,1)S(1)} collective-permute-done((bf16[512,512]{1,0:T(8,128)(2,1)S(1)}, bf16[512,512]{1,0:T(8,128)(2,1)S(1)}, u32[]{:S(2)}, u32[]{:S(2)}) %collective-permute-start.2) | collective-permute-done | bytes 524320 | tf_op jit(solution)/shard_map/ppermute | solution.py:66
  105.0 1.9 collective-permute-start.3
  106.9 6.7 %collective-permute-done.3 = bf16[512,512]{1,0:T(8,128)(2,1)S(1)} collective-permute-done((bf16[512,512]{1,0:T(8,128)(2,1)S(1)}, bf16[512,512]{1,0:T(8,128)(2,1)S(1)}, u32[]{:S(2)}, u32[]{:S(2)}) %collective-permute-start.3) | collective-permute-done | bytes 524320 | tf_op jit(solution)/shard_map/ppermute | solution.py:66
  113.6 1.9 collective-permute-start.4
  115.5 0.8 constant_dynamic-update-slice_fusion.6
  116.3 0.9 constant_dynamic-update-slice_fusion.5
  117.2 5.0 %collective-permute-done.4 = bf16[512,512]{1,0:T(8,128)(2,1)S(1)} collective-permute-done((bf16[512,512]{1,0:T(8,128)(2,1)S(1)}, bf16[512,512]{1,0:T(8,128)(2,1)S(1)}, u32[]{:S(2)}, u32[]{:S(2)}) %collective-permute-start.4) | collective-permute-done | bytes 524320 | tf_op jit(solution)/shard_map/ppermute | solution.py:66
  122.2 0.8 constant_dynamic-update-slice_fusion.4
  123.0 0.9 constant_dynamic-update-slice_fusion.3
  123.9 0.8 constant_dynamic-update-slice_fusion.2
  124.7 0.8 constant_dynamic-update-slice_fusion.1
  125.5 0.9 constant_dynamic-update-slice_fusion
  126.4 0.0 copy-done.4
  126.4 18.1 %convolution_bitcast_fusion = f32[2048,512]{0,1:T(8,128)} fusion(bf16[2048,2048]{1,0:T(8,128)(2,1)} %param.17, bf16[2048,2048]{1,0:T(8,128)(2,1)} %param.15, f32[2048]{0:T(1024)S(1)} %copy-done.4, bf16[4096,512]{1,0:T(8,128)(2,1)} %constant_dynamic-update-slice_fusion, s32[]{:T(128)S(6)} %select_n.19), kind=kOutput, calls=%fused_computation.51 | convolution fusion | flops 8600420352 | bytes 23076868 | tf_op jit(solution)/shard_map/dot_general | solution.py:79
  144.5 0.0 copy-start
  144.5 0.0 copy-start.1
  144.5 0.0 copy-start.2
  144.5 0.0 reduce-scatter.2.cloned.1.call-update
  144.5 1.0 copy-done
  145.5 0.3 copy.11
  145.8 46.1 %reduce-scatter.2.cloned.1.call-done = f32[512,512]{0,1:T(8,128)} async-done(((f32[2048,512]{0,1:T(8,128)}), f32[512,512]{0,1:T(8,128)}) %reduce-scatter.2.cloned.1.call-update) | async-done | bytes 1048592 | tf_op jit(solution)/shard_map/reduce_scatter | solution.py:80
  192.0 0.0 copy-done.1
  192.0 0.0 copy-done.2
  192.0 1.5 fusion.103
  193.5 1.1 copy.12
  (1 shorter events, 0.0 us)
Async XLA Ops:
  6.5 31.2 %copy-start.3 = (f32[512]{0:T(512)S(1)}, f32[512]{0:T(512)}, u32[]{:S(2)}) copy-start(f32[512]{0:T(512)} %param.12) | copy-start | bytes 6148
  6.5 185.4 %reduce-scatter.2.cloned.1.call-start = ((), (), s32[]{:S(2)}) async-start(), calls=%async_computation.1 | async-start | bytes 5242880 | tf_op jit(solution)/shard_map/reduce_scatter | solution.py:80
  8.2 27.3 %collective-permute-start = (bf16[512,3,128]{2,1,0:T(4,128)(2,1)S(1)}, bf16[512,3,128]{2,1,0:T(4,128)(2,1)S(1)}, u32[]{:S(2)}, u32[]{:S(2)}) collective-permute-start(bf16[512,3,128]{2,1,0:T(4,128)(2,1)S(1)} %get-tuple-element.12), channel_id=1, source_target_pairs={{0,1},{1,2},{2,3},{3,4},{4,5},{5,6},{6,7},{8,9},{9,10},{10,11},{11... | collective-permute-start | bytes 1179656 | tf_op jit(solution)/shard_map/ppermute | solution.py:14
  13.1 22.4 %collective-permute-start.1 = (bf16[512,3,128]{2,1,0:T(4,128)(2,1)S(1)}, bf16[512,3,128]{2,1,0:T(4,128)(2,1)S(1)}, u32[]{:S(2)}, u32[]{:S(2)}) collective-permute-start(bf16[512,3,128]{2,1,0:T(4,128)(2,1)S(1)} %get-tuple-element.13), channel_id=1, source_target_pairs={{1,0},{2,1},{3,2},{4,3},{5,4},{6,5},{7,6},{9,8},{10,9},{11,10},{12... | collective-permute-start | bytes 1179656 | tf_op jit(solution)/shard_map/ppermute | solution.py:17
  97.4 29.0 %copy-start.4 = (f32[2048]{0:T(1024)S(1)}, f32[2048]{0:T(1024)}, u32[]{:S(2)}) copy-start(f32[2048]{0:T(1024)} %param.16) | copy-start | bytes 24580
  97.4 7.6 %collective-permute-start.2 = (bf16[512,512]{1,0:T(8,128)(2,1)S(1)}, bf16[512,512]{1,0:T(8,128)(2,1)S(1)}, u32[]{:S(2)}, u32[]{:S(2)}) collective-permute-start(bf16[512,512]{1,0:T(8,128)(2,1)S(1)} %get-tuple-element.10), channel_id=1, source_target_pairs={{0,24},{8,0},{16,8},{24,16},{1,25},{9,1},{17,9},{25,17},{2,26},{10... | collective-permute-start | bytes 1572872 | tf_op jit(solution)/shard_map/ppermute | solution.py:66
  105.0 8.6 %collective-permute-start.3 = (bf16[512,512]{1,0:T(8,128)(2,1)S(1)}, bf16[512,512]{1,0:T(8,128)(2,1)S(1)}, u32[]{:S(2)}, u32[]{:S(2)}) collective-permute-start(bf16[512,512]{1,0:T(8,128)(2,1)S(1)} %collective-permute-done.2), channel_id=1, source_target_pairs={{0,24},{8,0},{16,8},{24,16},{1,25},{9,1},{17,9},{25,17},{2,26},{10... | collective-permute-start | bytes 1572872 | tf_op jit(solution)/shard_map/ppermute | solution.py:66
  113.6 8.6 %collective-permute-start.4 = (bf16[512,512]{1,0:T(8,128)(2,1)S(1)}, bf16[512,512]{1,0:T(8,128)(2,1)S(1)}, u32[]{:S(2)}, u32[]{:S(2)}) collective-permute-start(bf16[512,512]{1,0:T(8,128)(2,1)S(1)} %collective-permute-done.3), channel_id=1, source_target_pairs={{0,24},{8,0},{16,8},{24,16},{1,25},{9,1},{17,9},{25,17},{2,26},{10... | collective-permute-start | bytes 1572872 | tf_op jit(solution)/shard_map/ppermute | solution.py:66
  144.5 1.0 copy-start
  144.5 47.5 %copy-start.1 = (f32[512]{0:T(512)S(1)}, f32[512]{0:T(512)}, u32[]{:S(2)}) copy-start(f32[512]{0:T(512)} %param.18) | copy-start | bytes 6148
  144.5 47.5 %copy-start.2 = (f32[512]{0:T(512)S(1)}, f32[512]{0:T(512)}, u32[]{:S(2)}) copy-start(f32[512]{0:T(512)} %param.19) | copy-start | bytes 6148
Sparse Core Ops, SparseCore 0:
  144.6 47.3 reduce-scatter.1
